TPU v7x, 32 devices: a whole 2x2x4 slice. The times are simulated.
32 devices in a mesh: section: 8 (over z, y), dp: 4 (over x, core).
Axes of the slice: x: 2, y: 2, z: 4, core: 2. Of those that a mesh axis runs over, the one named last changes fastest.
Arguments:
- acts: bfloat16 [8, 2, 256, 6144], P('section', None, 'dp'), may hold values from -6 to 6
- grads_sent: bfloat16 [8, 2, 256, 6144], P('section', None, 'dp'), may hold values from -48 to 48
- replicas: bfloat16 [8, 2, 2, 16, 6144], P('section'), may hold values from -4 to 4
- master: float32 [8, 2, 16, 6144], P('section', None, None, 'dp'), may hold values from -1 to 1
- moment: float32 [8, 2, 16, 6144], P('section', None, None, 'dp'), may hold values from -3 to 3
- second: float32 [8, 2, 16, 6144], P('section', None, None, 'dp'), may hold values from 0.05 to 4
Outputs:
- new_master: float32 [8, 2, 16, 6144], P('section', None, None, 'dp')
- new_moment: float32 [8, 2, 16, 6144], P('section', None, None, 'dp')
- new_second: float32 [8, 2, 16, 6144], P('section', None, None, 'dp')
- new_replicas: bfloat16 [8, 2, 2, 16, 6144], P('section')
All inputs are finite; a program needn't handle non-finite values.
Results may differ from a plain program's by a relative error of at most 0.006.
Values may be sent and summed in bfloat16 or wider, within the bound.
A program may use at most 64 MiB of HBM per device.

v0:
```python
import jax
import jax.numpy as jnp
from jax import lax
from jax.sharding import PartitionSpec as P

D = 6144
FF = 24576


beta_one = 0.9
beta_two = 0.95
adam_eps = 1e-08
learn_rate = 0.05
decay_rate = 0.01
adam_steps = 10.0


def partner(value, axis, distance):
    mask = 2**distance
    pairs = [(source, source ^ mask) for source in range(lax.axis_size(axis))]
    return lax.ppermute(value, axis, pairs)


def shifted(block, axis, distance):
    devices = range(lax.axis_size(axis))
    route = [((i - distance) % len(devices), i) for i in devices]
    return lax.ppermute(block, axis, route)


def gelu_exact(values):
    return 0.5 * values * (1.0 + lax.erf(values * 0.7071067811865476))


def gelu_slope(values):
    return (
        0.5 * (1.0 + lax.erf(values * 0.7071067811865476))
        + values * jnp.exp(-0.5 * values * values) * 0.3989422804014327
    )


def forward_part(inputs, w_in):
    inv_width = 1.0 / D**0.5
    pre_act = (
        lax.dot_general(inputs, w_in, (((1,), (1,)), ((), ())), preferred_element_type=jnp.float32)
        * inv_width
    )
    activation = gelu_exact(pre_act).astype(jnp.bfloat16)
    return (pre_act, activation)


def upstream_part(upstream, w_out, activation):
    inv_hidden = 1.0 / FF**0.5
    act_grad = (
        lax.dot_general(
            upstream, w_out, (((1,), (1,)), ((), ())), preferred_element_type=jnp.float32
        )
        * inv_hidden
    )
    term_out = (
        lax.dot_general(
            activation, upstream, (((0,), (0,)), ((), ())), preferred_element_type=jnp.float32
        )
        * inv_hidden
    )
    return (act_grad, term_out)


def finish_part(inputs, pre_act, act_grad):
    inv_width = 1.0 / D**0.5
    pre_grad = (act_grad * gelu_slope(pre_act)).astype(jnp.bfloat16)
    return (
        lax.dot_general(
            pre_grad, inputs, (((0,), (0,)), ((), ())), preferred_element_type=jnp.float32
        )
        * inv_width
    )


def mirror_grads_move(payload):
    for bit_place in range(lax.axis_size("section").bit_length() - 1):
        payload = partner(payload.astype(jnp.bfloat16), "section", bit_place).astype(payload.dtype)
    return payload


def mirror_params_move(payload):
    for bit_place in range(lax.axis_size("section").bit_length() - 1):
        payload = partner(payload, "section", bit_place)
    return payload


def collect_columns(payload):
    return lax.all_gather(payload, "dp", axis=3, tiled=True)


def body(acts, grads_sent, replicas, master, moment, second):
    sections = lax.axis_size("section")
    worker = lax.axis_index("section")
    upper_half = worker >= sections // 2
    pre_down, act_down = forward_part(acts[0, 0], replicas[0, 0, 0])
    pre_up, act_up = forward_part(acts[0, 1], replicas[0, 1, 0])
    got_down = shifted((replicas[0, 0, 1], act_down), "section", 1)
    down_local = upstream_part(grads_sent[0, 0], got_down[0], got_down[1])
    back_down = (
        shifted(down_local[0].astype(jnp.bfloat16), "section", -1).astype(jnp.float32),
        shifted(down_local[1].astype(jnp.bfloat16), "section", -1).astype(jnp.float32),
    )
    got_up = shifted((replicas[0, 1, 1], act_up), "section", -1)
    up_local = upstream_part(grads_sent[0, 1], got_up[0], got_up[1])
    back_up = (
        shifted(up_local[0].astype(jnp.bfloat16), "section", 1).astype(jnp.float32),
        shifted(up_local[1].astype(jnp.bfloat16), "section", 1).astype(jnp.float32),
    )
    down_grad, down_out = back_down
    up_grad, up_out = back_up
    down_terms = jnp.stack([finish_part(acts[0, 0], pre_down, down_grad), down_out])
    up_terms = jnp.stack([finish_part(acts[0, 1], pre_up, up_grad), up_out])
    partials = jnp.stack([down_terms, up_terms])
    reduced = lax.psum_scatter(
        partials.astype(jnp.bfloat16), "dp", scatter_dimension=3, tiled=True
    ).astype(jnp.float32)
    own_part = jnp.where(upper_half, reduced[:, 1], reduced[:, 0])
    other_part = jnp.where(upper_half, reduced[:, 0], reduced[:, 1])
    arrived = mirror_grads_move(other_part)
    summed_grads = own_part + arrived[::-1]
    moment_now = beta_one * moment[0] + (1.0 - beta_one) * summed_grads
    second_now = beta_two * second[0] + (1.0 - beta_two) * summed_grads * summed_grads
    corrected = (
        moment_now
        / (1.0 - beta_one**adam_steps)
        / (jnp.sqrt(second_now / (1.0 - beta_two**adam_steps)) + adam_eps)
    )
    master_now = master[0] - learn_rate * (corrected + decay_rate * master[0])
    rounded = master_now.astype(jnp.bfloat16)
    from_mirror = mirror_params_move(rounded)
    combined = jnp.stack([rounded, from_mirror[::-1]])
    complete = collect_columns(combined)
    own_full = complete[0]
    other_full = complete[1]
    proj_in = jnp.where(upper_half, other_full, own_full)
    proj_out = jnp.where(upper_half, own_full, other_full)
    new_replicas = jnp.stack([proj_in, proj_out], axis=1)[None]
    return (master_now[None], moment_now[None], second_now[None], new_replicas)


def solution(mesh):
    in_specs = (
        P("section", None, "dp", None),
        P("section", None, "dp", None),
        P("section", None, None, None, None),
        P("section", None, None, "dp"),
        P("section", None, None, "dp"),
        P("section", None, None, "dp"),
    )
    out_specs = (
        P("section", None, None, "dp"),
        P("section", None, None, "dp"),
        P("section", None, None, "dp"),
        P("section", None, None, None, None),
    )
    return jax.shard_map(body, mesh=mesh, in_specs=in_specs, out_specs=out_specs, check_vma=False)
```

profile of v0, /device:TPU:0, one launch (start us, length us, event | category | flops | bytes accessed | tf_op | source)
XLA Modules:
  0.0 106.6 jit_solution(10803302405834282489)
XLA Ops:
  7.2 1.2 %slice_bitcast_fusion.1 = (bf16[16,6144]{1,0:T(8,128)(2,1)S(1)}, bf16[16,6144]{1,0:T(8,128)(2,1)S(1)}) fusion(bf16[1,2,2,16,6144]{4,3,2,1,0:T(8,128)(2,1)} %param.8), kind=kLoop, calls=%fused_computation.55 | loop fusion | bytes 786432 | tf_op jit(solution)/shard_map/squeeze | solution.py:101
  8.4 3.0 %collective-permute-start = (bf16[16,6144]{1,0:T(8,128)(2,1)S(1)}, bf16[16,6144]{1,0:T(8,128)(2,1)S(1)}, u32[]{:S(2)}, u32[]{:S(2)}) collective-permute-start(bf16[16,6144]{1,0:T(8,128)(2,1)S(1)} %get-tuple-element.13), channel_id=1, source_target_pairs={{28,0},{0,4},{4,8},{8,12},{12,16},{16,20},{20,24},{24,28},{29,1},{... | collective-permute-start | bytes 589832 | tf_op jit(solution)/shard_map/ppermute | solution.py:27
  11.5 1.5 %multiply_convert_fusion.2 = (bf16[64,16]{0,1:T(8,128)(2,1)S(1)}, f32[64,16]{0,1:T(8,128)S(1)}) fusion(bf16[1,2,2,16,6144]{4,3,2,1,0:T(8,128)(2,1)} %param.8, bf16[1,2,64,6144]{3,2,1,0:T(8,128)(2,1)} %param.6), kind=kOutput, calls=%fused_computation.63 | convolution fusion | flops 12588032 | bytes 989184 | tf_op jit(solution)/shard_map/dot_general | solution.py:44
  13.0 1.6 %collective-permute-start.2 = (bf16[64,16]{0,1:T(8,128)(2,1)S(1)}, bf16[64,16]{0,1:T(8,128)(2,1)S(1)}, u32[]{:S(2)}, u32[]{:S(2)}) collective-permute-start(bf16[64,16]{0,1:T(8,128)(2,1)S(1)} %get-tuple-element.19), channel_id=1, source_target_pairs={{28,0},{0,4},{4,8},{8,12},{12,16},{16,20},{20,24},{24,28},{29,1},{... | collective-permute-start | bytes 6152 | tf_op jit(solution)/shard_map/ppermute | solution.py:27
  14.5 3.2 %collective-permute-start.4 = (bf16[16,6144]{1,0:T(8,128)(2,1)S(1)}, bf16[16,6144]{1,0:T(8,128)(2,1)S(1)}, u32[]{:S(2)}, u32[]{:S(2)}) collective-permute-start(bf16[16,6144]{1,0:T(8,128)(2,1)S(1)} %get-tuple-element.14), channel_id=1, source_target_pairs={{4,0},{8,4},{12,8},{16,12},{20,16},{24,20},{28,24},{0,28},{5,1},{9... | collective-permute-start | bytes 589832 | tf_op jit(solution)/shard_map/ppermute | solution.py:27
  17.7 1.2 %multiply_convert_fusion = (bf16[64,16]{0,1:T(8,128)(2,1)S(1)}, f32[64,16]{0,1:T(8,128)S(1)}) fusion(bf16[1,2,2,16,6144]{4,3,2,1,0:T(8,128)(2,1)} %param.8, bf16[1,2,64,6144]{3,2,1,0:T(8,128)(2,1)S(1)} %copy-done.1), kind=kOutput, calls=%fused_computation.60 | convolution fusion | flops 12588032 | bytes 989184 | tf_op jit(solution)/shard_map/dot_general | solution.py:44
  19.8 2.7 %collective-permute-start.3 = (bf16[16,6144]{1,0:T(8,128)(2,1)S(1)}, bf16[16,6144]{1,0:T(8,128)(2,1)S(1)}, u32[]{:S(2)}, u32[]{:S(2)}) collective-permute-start(bf16[16,6144]{1,0:T(8,128)(2,1)S(1)} %fusion.1), channel_id=1, source_target_pairs={{4,0},{8,4},{12,8},{16,12},{20,16},{24,20},{28,24},{0,28},{5,1},{9... | collective-permute-start | bytes 589832 | tf_op jit(solution)/shard_map/ppermute | solution.py:27
  22.5 1.4 %collective-permute-done.6 = bf16[64,16]{0,1:T(8,128)(2,1)S(1)} collective-permute-done((bf16[64,16]{0,1:T(8,128)(2,1)S(1)}, bf16[64,16]{0,1:T(8,128)(2,1)S(1)}, u32[]{:S(2)}, u32[]{:S(2)}) %collective-permute-start.6) | collective-permute-done | bytes 2080 | tf_op jit(solution)/shard_map/ppermute | solution.py:27
  24.5 4.7 %collective-permute-start.1 = (bf16[64,16]{0,1:T(8,128)(2,1)S(1)}, bf16[64,16]{0,1:T(8,128)(2,1)S(1)}, u32[]{:S(2)}, u32[]{:S(2)}) collective-permute-start(bf16[64,16]{0,1:T(8,128)(2,1)S(1)} %fusion.6), channel_id=1, source_target_pairs={{4,0},{8,4},{12,8},{16,12},{20,16},{24,20},{28,24},{0,28},{5,1},{9... | collective-permute-start | bytes 6152 | tf_op jit(solution)/shard_map/ppermute | solution.py:27
  29.6 1.0 collective-permute-done.1
  30.9 5.0 %collective-permute-done.5 = bf16[64,16]{0,1:T(8,128)(2,1)S(1)} collective-permute-done((bf16[64,16]{0,1:T(8,128)(2,1)S(1)}, bf16[64,16]{0,1:T(8,128)(2,1)S(1)}, u32[]{:S(2)}, u32[]{:S(2)}) %collective-permute-start.5) | collective-permute-done | bytes 2080 | tf_op jit(solution)/shard_map/ppermute | solution.py:27
  37.2 20.6 %reduce-scatter.2.cloned.1.call-done = bf16[2,2,16,1536]{3,2,1,0:T(8,128)(2,1)} async-done(((bf16[2,2,16,6144]{3,2,1,0:T(8,128)(2,1)}), bf16[2,2,16,1536]{3,2,1,0:T(8,128)(2,1)}) %reduce-scatter.2.cloned.1.call-update) | async-done | bytes 196624 | tf_op jit(solution)/shard_map/reduce_scatter | solution.py:118
  58.8 1.5 %collective-permute-start.8 = (bf16[2,16,1536]{2,1,0:T(8,128)(2,1)S(1)}, bf16[2,16,1536]{2,1,0:T(8,128)(2,1)S(1)}, u32[]{:S(2)}, u32[]{:S(2)}) collective-permute-start(bf16[2,16,1536]{2,1,0:T(8,128)(2,1)S(1)} %fusion.35), channel_id=1, source_target_pairs={{0,4},{4,0},{8,12},{12,8},{16,20},{20,16},{24,28},{28,24},{1,5},{5... | collective-permute-start | bytes 294920 | tf_op jit(solution)/shard_map/ppermute | solution.py:21
  60.4 3.1 %collective-permute-done.8 = bf16[2,16,1536]{2,1,0:T(8,128)(2,1)S(1)} collective-permute-done((bf16[2,16,1536]{2,1,0:T(8,128)(2,1)S(1)}, bf16[2,16,1536]{2,1,0:T(8,128)(2,1)S(1)}, u32[]{:S(2)}, u32[]{:S(2)}) %collective-permute-start.8) | collective-permute-done | bytes 98336 | tf_op jit(solution)/shard_map/ppermute | solution.py:21
  63.5 1.5 %collective-permute-start.9 = (bf16[2,16,1536]{2,1,0:T(8,128)(2,1)S(1)}, bf16[2,16,1536]{2,1,0:T(8,128)(2,1)S(1)}, u32[]{:S(2)}, u32[]{:S(2)}) collective-permute-start(bf16[2,16,1536]{2,1,0:T(8,128)(2,1)S(1)} %collective-permute-done.8), channel_id=1, source_target_pairs={{0,8},{4,12},{8,0},{12,4},{16,24},{20,28},{24,16},{28,20},{1,9},{5... | collective-permute-start | bytes 294920 | tf_op jit(solution)/shard_map/ppermute | solution.py:21
  65.0 3.1 %collective-permute-done.9 = bf16[2,16,1536]{2,1,0:T(8,128)(2,1)S(1)} collective-permute-done((bf16[2,16,1536]{2,1,0:T(8,128)(2,1)S(1)}, bf16[2,16,1536]{2,1,0:T(8,128)(2,1)S(1)}, u32[]{:S(2)}, u32[]{:S(2)}) %collective-permute-start.9) | collective-permute-done | bytes 98336 | tf_op jit(solution)/shard_map/ppermute | solution.py:21
  68.1 2.5 %collective-permute-start.10 = (bf16[2,16,1536]{2,1,0:T(8,128)(2,1)S(1)}, bf16[2,16,1536]{2,1,0:T(8,128)(2,1)S(1)}, u32[]{:S(2)}, u32[]{:S(2)}) collective-permute-start(bf16[2,16,1536]{2,1,0:T(8,128)(2,1)S(1)} %collective-permute-done.9), channel_id=1, source_target_pairs={{0,16},{4,20},{8,24},{12,28},{16,0},{20,4},{24,8},{28,12},{1,17},{... | collective-permute-start | bytes 294920 | tf_op jit(solution)/shard_map/ppermute | solution.py:21
  70.6 4.1 %collective-permute-done.10 = bf16[2,16,1536]{2,1,0:T(8,128)(2,1)S(1)} collective-permute-done((bf16[2,16,1536]{2,1,0:T(8,128)(2,1)S(1)}, bf16[2,16,1536]{2,1,0:T(8,128)(2,1)S(1)}, u32[]{:S(2)}, u32[]{:S(2)}) %collective-permute-start.10) | collective-permute-done | bytes 98336 | tf_op jit(solution)/shard_map/ppermute | solution.py:21
  75.6 1.5 %collective-permute-start.11 = (bf16[2,16,1536]{2,1,0:T(8,128)(2,1)S(1)}, bf16[2,16,1536]{2,1,0:T(8,128)(2,1)S(1)}, u32[]{:S(2)}, u32[]{:S(2)}) collective-permute-start(bf16[2,16,1536]{2,1,0:T(8,128)(2,1)S(1)} %get-tuple-element.8), channel_id=1, source_target_pairs={{0,4},{4,0},{8,12},{12,8},{16,20},{20,16},{24,28},{28,24},{1,5},{5... | collective-permute-start | bytes 294920 | tf_op jit(solution)/shard_map/ppermute | solution.py:21
  77.1 3.1 %collective-permute-done.11 = bf16[2,16,1536]{2,1,0:T(8,128)(2,1)S(1)} collective-permute-done((bf16[2,16,1536]{2,1,0:T(8,128)(2,1)S(1)}, bf16[2,16,1536]{2,1,0:T(8,128)(2,1)S(1)}, u32[]{:S(2)}, u32[]{:S(2)}) %collective-permute-start.11) | collective-permute-done | bytes 98336 | tf_op jit(solution)/shard_map/ppermute | solution.py:21
  80.8 4.1 %collective-permute-done.12 = bf16[2,16,1536]{2,1,0:T(8,128)(2,1)S(1)} collective-permute-done((bf16[2,16,1536]{2,1,0:T(8,128)(2,1)S(1)}, bf16[2,16,1536]{2,1,0:T(8,128)(2,1)S(1)}, u32[]{:S(2)}, u32[]{:S(2)}) %collective-permute-start.12) | collective-permute-done | bytes 98336 | tf_op jit(solution)/shard_map/ppermute | solution.py:21
  84.9 1.9 %collective-permute-start.13 = (bf16[2,16,1536]{2,1,0:T(8,128)(2,1)S(1)}, bf16[2,16,1536]{2,1,0:T(8,128)(2,1)S(1)}, u32[]{:S(2)}, u32[]{:S(2)}) collective-permute-start(bf16[2,16,1536]{2,1,0:T(8,128)(2,1)S(1)} %collective-permute-done.12), channel_id=1, source_target_pairs={{0,16},{4,20},{8,24},{12,28},{16,0},{20,4},{24,8},{28,12},{1,17},{... | collective-permute-start | bytes 294920 | tf_op jit(solution)/shard_map/ppermute | solution.py:21
  87.6 3.9 %collective-permute-done.13 = bf16[2,16,1536]{2,1,0:T(8,128)(2,1)S(1)} collective-permute-done((bf16[2,16,1536]{2,1,0:T(8,128)(2,1)S(1)}, bf16[2,16,1536]{2,1,0:T(8,128)(2,1)S(1)}, u32[]{:S(2)}, u32[]{:S(2)}) %collective-permute-start.13) | collective-permute-done | bytes 98336 | tf_op jit(solution)/shard_map/ppermute | solution.py:21
  91.5 7.2 %all_gather.3 = bf16[2,2,16,6144]{3,2,1,0:T(8,128)(2,1)S(1)} all-gather(bf16[2,2,16,1536]{3,2,1,0:T(8,128)(2,1)S(1)} %pad_maximum_fusion.1), channel_id=1, replica_groups=mesh['section'=8,'dp'=4] {'dp'}, dimensions={3}, use_global_device_ids=true | all-gather | bytes 983040 | tf_op jit(solution)/shard_map/all_gather | solution.py:92
  (40 shorter events, 7.7 us)
Async XLA Ops:
  7.2 10.6 %copy-start.1 = (bf16[1,2,64,6144]{3,2,1,0:T(8,128)(2,1)S(1)}, bf16[1,2,64,6144]{3,2,1,0:T(8,128)(2,1)}, u32[]{:S(2)}) copy-start(bf16[1,2,64,6144]{3,2,1,0:T(8,128)(2,1)} %param.6) | copy-start | bytes 4718596
  7.2 12.4 %copy-start = (bf16[1,2,64,6144]{3,2,1,0:T(8,128)(2,1)S(1)}, bf16[1,2,64,6144]{3,2,1,0:T(8,128)(2,1)}, u32[]{:S(2)}) copy-start(bf16[1,2,64,6144]{3,2,1,0:T(8,128)(2,1)} %param.7) | copy-start | bytes 4718596
  7.2 50.6 %reduce-scatter.2.cloned.1.call-start = ((), (), s32[]{:S(2)}) async-start(), calls=%async_computation.1 | async-start | bytes 983040 | tf_op jit(solution)/shard_map/reduce_scatter | solution.py:118
  8.4 15.8 %collective-permute-start = (bf16[16,6144]{1,0:T(8,128)(2,1)S(1)}, bf16[16,6144]{1,0:T(8,128)(2,1)S(1)}, u32[]{:S(2)}, u32[]{:S(2)}) collective-permute-start(bf16[16,6144]{1,0:T(8,128)(2,1)S(1)} %get-tuple-element.13), channel_id=1, source_target_pairs={{28,0},{0,4},{4,8},{8,12},{12,16},{16,20},{20,24},{24,28},{29,1},{... | collective-permute-start | bytes 589832 | tf_op jit(solution)/shard_map/ppermute | solution.py:27
  13.0 6.7 %collective-permute-start.2 = (bf16[64,16]{0,1:T(8,128)(2,1)S(1)}, bf16[64,16]{0,1:T(8,128)(2,1)S(1)}, u32[]{:S(2)}, u32[]{:S(2)}) collective-permute-start(bf16[64,16]{0,1:T(8,128)(2,1)S(1)} %get-tuple-element.19), channel_id=1, source_target_pairs={{28,0},{0,4},{4,8},{8,12},{12,16},{16,20},{20,24},{24,28},{29,1},{... | collective-permute-start | bytes 6152 | tf_op jit(solution)/shard_map/ppermute | solution.py:27
  14.5 14.7 %collective-permute-start.4 = (bf16[16,6144]{1,0:T(8,128)(2,1)S(1)}, bf16[16,6144]{1,0:T(8,128)(2,1)S(1)}, u32[]{:S(2)}, u32[]{:S(2)}) collective-permute-start(bf16[16,6144]{1,0:T(8,128)(2,1)S(1)} %get-tuple-element.14), channel_id=1, source_target_pairs={{4,0},{8,4},{12,8},{16,12},{20,16},{24,20},{28,24},{0,28},{5,1},{9... | collective-permute-start | bytes 589832 | tf_op jit(solution)/shard_map/ppermute | solution.py:27
  19.0 4.9 %collective-permute-start.6 = (bf16[64,16]{0,1:T(8,128)(2,1)S(1)}, bf16[64,16]{0,1:T(8,128)(2,1)S(1)}, u32[]{:S(2)}, u32[]{:S(2)}) collective-permute-start(bf16[64,16]{0,1:T(8,128)(2,1)S(1)} %get-tuple-element.17), channel_id=1, source_target_pairs={{4,0},{8,4},{12,8},{16,12},{20,16},{24,20},{28,24},{0,28},{5,1},{9... | collective-permute-start | bytes 6152 | tf_op jit(solution)/shard_map/ppermute | solution.py:27
  19.8 11.0 %collective-permute-start.3 = (bf16[16,6144]{1,0:T(8,128)(2,1)S(1)}, bf16[16,6144]{1,0:T(8,128)(2,1)S(1)}, u32[]{:S(2)}, u32[]{:S(2)}) collective-permute-start(bf16[16,6144]{1,0:T(8,128)(2,1)S(1)} %fusion.1), channel_id=1, source_target_pairs={{4,0},{8,4},{12,8},{16,12},{20,16},{24,20},{28,24},{0,28},{5,1},{9... | collective-permute-start | bytes 589832 | tf_op jit(solution)/shard_map/ppermute | solution.py:27
  24.1 12.0 %collective-permute-start.7 = (bf16[16,6144]{1,0:T(8,128)(2,1)S(1)}, bf16[16,6144]{1,0:T(8,128)(2,1)S(1)}, u32[]{:S(2)}, u32[]{:S(2)}) collective-permute-start(bf16[16,6144]{1,0:T(8,128)(2,1)S(1)} %fusion.3), channel_id=1, source_target_pairs={{28,0},{0,4},{4,8},{8,12},{12,16},{16,20},{20,24},{24,28},{29,1},{... | collective-permute-start | bytes 589832 | tf_op jit(solution)/shard_map/ppermute | solution.py:27
  24.5 6.0 %collective-permute-start.1 = (bf16[64,16]{0,1:T(8,128)(2,1)S(1)}, bf16[64,16]{0,1:T(8,128)(2,1)S(1)}, u32[]{:S(2)}, u32[]{:S(2)}) collective-permute-start(bf16[64,16]{0,1:T(8,128)(2,1)S(1)} %fusion.6), channel_id=1, source_target_pairs={{4,0},{8,4},{12,8},{16,12},{20,16},{24,20},{28,24},{0,28},{5,1},{9... | collective-permute-start | bytes 6152 | tf_op jit(solution)/shard_map/ppermute | solution.py:27
  29.6 6.3 %collective-permute-start.5 = (bf16[64,16]{0,1:T(8,128)(2,1)S(1)}, bf16[64,16]{0,1:T(8,128)(2,1)S(1)}, u32[]{:S(2)}, u32[]{:S(2)}) collective-permute-start(bf16[64,16]{0,1:T(8,128)(2,1)S(1)} %fusion.7), channel_id=1, source_target_pairs={{28,0},{0,4},{4,8},{8,12},{12,16},{16,20},{20,24},{24,28},{29,1},{... | collective-permute-start | bytes 6152 | tf_op jit(solution)/shard_map/ppermute | solution.py:27
  36.2 38.5 %copy-start.2 = (f32[1,2,16,1536]{3,2,1,0:T(8,128)S(1)}, f32[1,2,16,1536]{3,2,1,0:T(8,128)}, u32[]{:S(2)}) copy-start(f32[1,2,16,1536]{3,2,1,0:T(8,128)} %param.11) | copy-start | bytes 589828
  36.2 38.5 %copy-start.3 = (f32[1,2,16,1536]{3,2,1,0:T(8,128)S(1)}, f32[1,2,16,1536]{3,2,1,0:T(8,128)}, u32[]{:S(2)}) copy-start(f32[1,2,16,1536]{3,2,1,0:T(8,128)} %param.10) | copy-start | bytes 589828
  36.2 38.5 %copy-start.4 = (f32[1,2,16,1536]{3,2,1,0:T(8,128)S(1)}, f32[1,2,16,1536]{3,2,1,0:T(8,128)}, u32[]{:S(2)}) copy-start(f32[1,2,16,1536]{3,2,1,0:T(8,128)} %param.9) | copy-start | bytes 589828
  58.8 4.7 %collective-permute-start.8 = (bf16[2,16,1536]{2,1,0:T(8,128)(2,1)S(1)}, bf16[2,16,1536]{2,1,0:T(8,128)(2,1)S(1)}, u32[]{:S(2)}, u32[]{:S(2)}) collective-permute-start(bf16[2,16,1536]{2,1,0:T(8,128)(2,1)S(1)} %fusion.35), channel_id=1, source_target_pairs={{0,4},{4,0},{8,12},{12,8},{16,20},{20,16},{24,28},{28,24},{1,5},{5... | collective-permute-start | bytes 294920 | tf_op jit(solution)/shard_map/ppermute | solution.py:21
  63.5 4.6 %collective-permute-start.9 = (bf16[2,16,1536]{2,1,0:T(8,128)(2,1)S(1)}, bf16[2,16,1536]{2,1,0:T(8,128)(2,1)S(1)}, u32[]{:S(2)}, u32[]{:S(2)}) collective-permute-start(bf16[2,16,1536]{2,1,0:T(8,128)(2,1)S(1)} %collective-permute-done.8), channel_id=1, source_target_pairs={{0,8},{4,12},{8,0},{12,4},{16,24},{20,28},{24,16},{28,20},{1,9},{5... | collective-permute-start | bytes 294920 | tf_op jit(solution)/shard_map/ppermute | solution.py:21
  68.1 6.6 %collective-permute-start.10 = (bf16[2,16,1536]{2,1,0:T(8,128)(2,1)S(1)}, bf16[2,16,1536]{2,1,0:T(8,128)(2,1)S(1)}, u32[]{:S(2)}, u32[]{:S(2)}) collective-permute-start(bf16[2,16,1536]{2,1,0:T(8,128)(2,1)S(1)} %collective-permute-done.9), channel_id=1, source_target_pairs={{0,16},{4,20},{8,24},{12,28},{16,0},{20,4},{24,8},{28,12},{1,17},{... | collective-permute-start | bytes 294920 | tf_op jit(solution)/shard_map/ppermute | solution.py:21
  75.6 4.6 %collective-permute-start.11 = (bf16[2,16,1536]{2,1,0:T(8,128)(2,1)S(1)}, bf16[2,16,1536]{2,1,0:T(8,128)(2,1)S(1)}, u32[]{:S(2)}, u32[]{:S(2)}) collective-permute-start(bf16[2,16,1536]{2,1,0:T(8,128)(2,1)S(1)} %get-tuple-element.8), channel_id=1, source_target_pairs={{0,4},{4,0},{8,12},{12,8},{16,20},{20,16},{24,28},{28,24},{1,5},{5... | collective-permute-start | bytes 294920 | tf_op jit(solution)/shard_map/ppermute | solution.py:21
  80.2 4.7 %collective-permute-start.12 = (bf16[2,16,1536]{2,1,0:T(8,128)(2,1)S(1)}, bf16[2,16,1536]{2,1,0:T(8,128)(2,1)S(1)}, u32[]{:S(2)}, u32[]{:S(2)}) collective-permute-start(bf16[2,16,1536]{2,1,0:T(8,128)(2,1)S(1)} %collective-permute-done.11), channel_id=1, source_target_pairs={{0,8},{4,12},{8,0},{12,4},{16,24},{20,28},{24,16},{28,20},{1,9},{5... | collective-permute-start | bytes 294920 | tf_op jit(solution)/shard_map/ppermute | solution.py:21
  84.9 6.6 %collective-permute-start.13 = (bf16[2,16,1536]{2,1,0:T(8,128)(2,1)S(1)}, bf16[2,16,1536]{2,1,0:T(8,128)(2,1)S(1)}, u32[]{:S(2)}, u32[]{:S(2)}) collective-permute-start(bf16[2,16,1536]{2,1,0:T(8,128)(2,1)S(1)} %collective-permute-done.12), channel_id=1, source_target_pairs={{0,16},{4,20},{8,24},{12,28},{16,0},{20,4},{24,8},{28,12},{1,17},{... | collective-permute-start | bytes 294920 | tf_op jit(solution)/shard_map/ppermute | solution.py:21
Sparse Core Ops, SparseCore 0:
  37.3 20.4 reduce-scatter.1
where the time goes:
time: 107 us
  waiting for transfers between devices  49.8 us (47%)
  starting transfers between devices  25.2 us (24%)
  between operations  14.2 us (13%)
  blocking collectives  7.23 us (7%)
  matrix products  4.25 us (4%)
  other arithmetic  3.83 us (4%)
  local copies, waits for them, and re-layouts  2.17 us (2%)
    ppermute x6, waiting for transfers between devices, partner(): return lax.ppermute(value, axis, pairs)  21.5 us
    reduce_scatter x1, waiting for transfers between devices, body(): lax.psum_scatter(partials.astype(jnp.bfloat16), 'dp', scatter_dimension=3...  20.6 us
    ppermute x8, starting transfers between devices, shifted(): return lax.ppermute(block, axis, route)  15.7 us
    ppermute x6, starting transfers between devices, partner(): return lax.ppermute(value, axis, pairs)  9.44 us
    ppermute x8, waiting for transfers between devices, shifted(): return lax.ppermute(block, axis, route)  7.64 us
    all_gather x1, blocking collectives, collect_columns(): return lax.all_gather(payload, 'dp', axis=3, tiled=True)  7.23 us
    dot_general x2, matrix products, forward_part(): lax.dot_general(inputs, w_in, (((1,), (1,)), ((), ())), preferred_element...  2.71 us
  transfers between devices with their start and end apart: 15, of which 11 were waited for; matrix products, arithmetic and copies ran while one was open for 5% of the time, Pallas kernels for 0%

commit v1 on v0

v1 whole, which is shorter than its diff:
```python
import functools
import math

import jax
import jax.numpy as jnp
from jax import lax
from jax.experimental import pallas as pl
from jax.experimental.pallas import tpu as pltpu
from jax.sharding import PartitionSpec as P

FF = 24576

beta_one = 0.9
beta_two = 0.95
adam_eps = 1e-08
learn_rate = 0.05
decay_rate = 0.01
adam_steps = 10.0

MESH = pl.DeviceIdType.MESH
NT = (((1,), (1,)), ((), ()))
NN = (((1,), (0,)), ((), ()))


def gelu_exact(values):
    return 0.5 * values * (1.0 + lax.erf(values * 0.7071067811865476))


def gelu_slope(values):
    return (
        0.5 * (1.0 + lax.erf(values * 0.7071067811865476))
        + values * jnp.exp(-0.5 * values * values) * 0.3989422804014327
    )


def dot(a, b, dims):
    return lax.dot_general(a, b, dims, preferred_element_type=jnp.float32)


class Sems:
    def __init__(self, groups):
        self.base, at = {}, 0
        for name, count in groups:
            self.base[name] = at
            at += count
        self.total = at

    def __call__(self, name, k=0):
        return self.base[name] + k


def sem_plan(groups):
    return Sems(
        [
            ("wout", 2),
            ("pass", 2),
            ("act", 2),
            ("back", 2),
            ("pair", 4),
            ("cross", 4 * groups),
            ("owner", 4),
            ("mirror", 2),
            ("spread", 2 * groups),
            ("twin", 2 * groups),
        ]
    )


def kernel(
    S, N, acts, grads, reps, master, moment, second,
    o_master, o_moment, o_second, o_reps,
    acts_v, ups_v, win_v, wout_v, act_s, act_r, ag_s, ag_r,
    term_v, pair_v, x_s, x_r, own_s, own_r, opt_v, opt_o, rep_v,
    load, send, recv,
):
    G = N // 2
    D = acts.shape[-1]
    C = D // N
    H = D // 2
    half = S // 2
    inv_width = 1.0 / D**0.5
    inv_hidden = 1.0 / FF**0.5
    K = sem_plan(G)
    w = lax.axis_index("section")
    d = lax.axis_index("dp")
    g, core = lax.div(d, 2), lax.rem(d, 2)
    nxt, prv, mir = lax.rem(w + 1, S), lax.rem(w + S - 1, S), S - 1 - w
    upper = w >= half
    twin = (w, g * 2 + 1 - core)
    peers = {r: lax.rem(g + r, G) for r in range(1, G)}
    from_ = {r: lax.rem(g + G - r, G) for r in range(1, G)}

    def cols(n):
        return pl.ds(pl.multiple_of(n * C, 128), C)

    def rc(src, dst, k, dev, kr=None):
        return pltpu.make_async_remote_copy(
            src_ref=src, dst_ref=dst, send_sem=send.at[k],
            recv_sem=recv.at[k if kr is None else kr],
            device_id=dev, device_id_type=MESH,
        )

    barrier = pltpu.get_barrier_semaphore()
    greet = [(nxt, d), (prv, d), (mir, d), (S - 1 - nxt, d), (S - 1 - prv, d), twin]
    greet += [(w, peers[r] * 2 + core) for r in range(1, G)]
    for dev in greet:
        pl.semaphore_signal(barrier, inc=1, device_id=dev, device_id_type=MESH)

    loads = [pltpu.make_async_copy(reps.at[:, 0], win_v, load.at[0])]
    loads += [pltpu.make_async_copy(acts.at[c], acts_v.at[c], load.at[1 + c]) for c in range(2)]
    loads += [pltpu.make_async_copy(grads.at[c], ups_v.at[c], load.at[3 + c]) for c in range(2)]
    loads += [
        pltpu.make_async_copy(ref, opt_v.at[i], load.at[5 + i])
        for i, ref in enumerate((master, moment, second))
    ]
    for copy in loads:
        copy.start()
    pl.semaphore_wait(barrier, len(greet))

    sent = []

    def go(copy):
        copy.start()
        sent.append(copy)
        return copy

    ahead = [(nxt, d), (prv, d)]
    behind = [(prv, d), (nxt, d)]
    mine = pl.ds(pl.multiple_of(core * H, 128), H)
    wout = [
        go(rc(reps.at[c, 1, :, mine], wout_v.at[c, :, mine], K("wout", c), ahead[c]))
        for c in range(2)
    ]

    loads[0].wait()
    pre, act_c = [], []
    for c in range(2):
        loads[1 + c].wait()
        value = dot(win_v[c], acts_v[c], NT) * inv_width
        pre.append(value)
        act_s[c] = gelu_exact(value).astype(jnp.bfloat16)
        act_c.append(go(rc(act_s.at[c], act_r.at[c], K("act", c), ahead[c])))

    def put_term(t, value):
        value = value.astype(jnp.bfloat16)
        for n in range(N):
            term_v[n % 2, t, n // 2] = value[:, n * C : (n + 1) * C]
        return go(rc(term_v.at[1 - core, t], pair_v.at[t], K("pair", t), twin))

    pair = [None] * 4
    cross = [None] * 4
    held = [None] * 4

    def to_peers(t):
        pair[t].wait_recv()
        cross[t] = []
        for r in range(1, G):
            x_s[t, r] = (
                term_v[core, t, peers[r]].astype(jnp.float32)
                + pair_v[t, peers[r]].astype(jnp.float32)
            ).astype(jnp.bfloat16)
            cross[t].append(
                go(rc(x_s.at[t, r], x_r.at[t, r], K("cross", t * G + r), (w, peers[r] * 2 + core)))
            )

    def from_peers(t):
        total = term_v[core, t, g].astype(jnp.float32) + pair_v[t, g].astype(jnp.float32)
        for r in range(1, G):
            cross[t][r - 1].wait_recv()
            total = total + x_r[t, r].astype(jnp.float32)
        return total

    for c in range(2):
        loads[3 + c].wait()
        act_c[c].wait_recv()
        pair[2 + c] = put_term(2 + c, dot(act_r[c], ups_v[c], NN) * inv_hidden)

    passed = []
    for c in range(2):
        wout[c].wait_recv()
        passed.append(go(rc(wout_v.at[c, :, mine], wout_v.at[c, :, mine], K("pass", c), twin)))
    to_peers(2)
    to_peers(3)
    back = []
    for c in range(2):
        passed[c].wait_recv()
        ag_s[c] = dot(wout_v[c], ups_v[c], NT) * inv_hidden
        back.append(go(rc(ag_s.at[c], ag_r.at[c], K("back", c), behind[c])))

    low0, low1 = S - 1 - prv, S - 1 - nxt
    dest0 = jnp.where(prv >= half, prv, low0)
    slot0 = jnp.where(prv >= half, 0, 2)
    dest1 = jnp.where(nxt >= half, nxt, low1)
    slot1 = jnp.where(nxt >= half, 3, 1)
    own_s[2] = from_peers(2).astype(jnp.bfloat16)
    own_s[3] = from_peers(3).astype(jnp.bfloat16)
    out0 = rc(own_s.at[2], own_r.at[slot0], K("owner", 2), (dest0, d), K("owner", slot0))
    out1 = rc(own_s.at[3], own_r.at[slot1], K("owner", 3), (dest1, d), K("owner", slot1))

    @pl.when(dest0 != w)
    def _():
        out0.start()

    @pl.when(dest0 == w)
    def _():
        own_r[2] = own_s[2]

    @pl.when(dest1 != w)
    def _():
        out1.start()

    @pl.when(dest1 == w)
    def _():
        own_r[1] = own_s[3]

    for c in range(2):
        back[c].wait_recv()
        pre_grad = (ag_r[c] * gelu_slope(pre[c])).astype(jnp.bfloat16)
        pair[c] = put_term(c, dot(pre_grad, acts_v[c], NN) * inv_width)

    part = jnp.where(upper, 1, 0)
    mine_c = cols(d)

    def arrival(i):
        return rc(own_s.at[0], own_r.at[i], K("owner", i), (mir, d))

    def block(p, n):
        return rep_v.at[:, p, :, cols(n)]

    def share(p, which):
        here = block(p, d)
        return [rc(here, here, K("twin", which * G), twin)] + [
            rc(here, here, K("spread", which * G + r), (w, peers[r] * 2 + core))
            for r in range(1, G)
        ]

    mirror = [
        rc(rep_v.at[j, part, :, mine_c], rep_v.at[1 - j, part, :, mine_c], K("mirror", j), (mir, d))
        for j in range(2)
    ]
    own_share = share(part, 0)

    def update(owned):
        for j in range(2):
            grad = owned[j]
            master_0 = opt_v[0, j]
            moment_now = beta_one * opt_v[1, j] + (1.0 - beta_one) * grad
            second_now = beta_two * opt_v[2, j] + (1.0 - beta_two) * grad * grad
            corrected = (
                moment_now
                / (1.0 - beta_one**adam_steps)
                / (jnp.sqrt(second_now / (1.0 - beta_two**adam_steps)) + adam_eps)
            )
            master_now = master_0 - learn_rate * (corrected + decay_rate * master_0)
            rep_v[j, part, :, mine_c] = master_now.astype(jnp.bfloat16)
            mirror[j].start()
            opt_o[0, j] = master_now
            opt_o[1, j] = moment_now
            opt_o[2, j] = second_now
        for copy in own_share:
            copy.start()

    for i in range(3):
        loads[5 + i].wait()

    to_peers(0)
    to_peers(1)

    @pl.when(upper)
    def _():
        arrival(0).wait_recv()
        arrival(3).wait_recv()

        @pl.when(w != S - 1)
        def _():
            arrival(1).wait_recv()

        @pl.when(w != half)
        def _():
            arrival(2).wait_recv()

        update(
            [
                own_r[2 * j].astype(jnp.float32) + own_r[2 * j + 1].astype(jnp.float32)
                for j in range(2)
            ]
        )

    in0 = rc(own_s.at[0], own_r.at[1], K("owner", 0), (mir, d), K("owner", 1))
    in1 = rc(own_s.at[1], own_r.at[0], K("owner", 1), (mir, d), K("owner", 0))
    term0 = from_peers(0)
    term1 = from_peers(1)

    @pl.when(upper)
    def _():
        own_s[0] = term0.astype(jnp.bfloat16)
        own_s[1] = term1.astype(jnp.bfloat16)
        in0.start()
        in1.start()

    @pl.when(jnp.logical_not(upper))
    def _():
        arrival(0).wait_recv()
        arrival(1).wait_recv()
        update([term0 + own_r[0].astype(jnp.float32), term1 + own_r[1].astype(jnp.float32)])

    outs = [
        pltpu.make_async_copy(opt_o.at[i], ref, load.at[i])
        for i, ref in enumerate((o_master, o_moment, o_second))
    ]
    for copy in outs:
        copy.start()

    other = 1 - part
    far_share = share(other, 1)

    def forward(p, which):
        for r in range(1, G):
            n = from_[r] * 2 + core
            rc(block(p, n), block(p, n), K("spread", which * G + r), twin).wait_recv()
            go(rc(block(p, n), block(p, n), K("twin", which * G + r), twin))

    def take_far():
        for j in range(2):
            mirror[j].wait_recv()
        for copy in far_share:
            copy.start()

    take_far()
    forward(part, 0)
    forward(other, 1)
    for which, p in ((0, part), (1, other)):
        for r in range(G):
            n = (from_[r] if r else g) * 2 + 1 - core
            rc(block(p, n), block(p, n), K("twin", which * G + r), twin).wait_recv()
    last = pltpu.make_async_copy(rep_v, o_reps, load.at[3])
    last.start()

    for copy in sent + mirror + own_share + far_share:
        copy.wait_send()

    @pl.when(dest0 != w)
    def _():
        out0.wait_send()

    @pl.when(dest1 != w)
    def _():
        out1.wait_send()

    @pl.when(upper)
    def _():
        in0.wait_send()
        in1.wait_send()

    for copy in outs:
        copy.wait()
    last.wait()


def body(S, N, acts, grads_sent, replicas, master, moment, second):
    _, _, T, D = acts.shape
    U = replicas.shape[3]
    C = D // N
    G = N // 2
    bf, f32 = jnp.bfloat16, jnp.float32
    K = sem_plan(G)
    any_spec = pl.BlockSpec(memory_space=pl.ANY)
    outs = pl.pallas_call(
        functools.partial(kernel, S, N),
        out_shape=[
            jax.ShapeDtypeStruct((2, U, C), f32),
            jax.ShapeDtypeStruct((2, U, C), f32),
            jax.ShapeDtypeStruct((2, U, C), f32),
            jax.ShapeDtypeStruct((2, 2, U, D), bf),
        ],
        in_specs=[any_spec] * 6,
        out_specs=[any_spec] * 4,
        scratch_shapes=[
            pltpu.VMEM((2, T, D), bf),
            pltpu.VMEM((2, T, D), bf),
            pltpu.VMEM((2, U, D), bf),
            pltpu.VMEM((2, U, D), bf),
            pltpu.VMEM((2, U, T), bf),
            pltpu.VMEM((2, U, T), bf),
            pltpu.VMEM((2, U, T), f32),
            pltpu.VMEM((2, U, T), f32),
            pltpu.VMEM((2, 4, G, U, C), bf),
            pltpu.VMEM((4, G, U, C), bf),
            pltpu.VMEM((4, G, U, C), bf),
            pltpu.VMEM((4, G, U, C), bf),
            pltpu.VMEM((4, U, C), bf),
            pltpu.VMEM((4, U, C), bf),
            pltpu.VMEM((3, 2, U, C), f32),
            pltpu.VMEM((3, 2, U, C), f32),
            pltpu.VMEM((2, 2, U, D), bf),
            pltpu.SemaphoreType.DMA((8,)),
            pltpu.SemaphoreType.DMA((K.total,)),
            pltpu.SemaphoreType.DMA((K.total,)),
        ],
        compiler_params=pltpu.CompilerParams(collective_id=0, has_side_effects=True),
    )(acts[0], grads_sent[0], replicas[0], master[0], moment[0], second[0])
    return tuple(out[None] for out in outs)


def solution(mesh):
    in_specs = (
        P("section", None, "dp", None),
        P("section", None, "dp", None),
        P("section", None, None, None, None),
        P("section", None, None, "dp"),
        P("section", None, None, "dp"),
        P("section", None, None, "dp"),
    )
    out_specs = (
        P("section", None, None, "dp"),
        P("section", None, None, "dp"),
        P("section", None, None, "dp"),
        P("section", None, None, None, None),
    )
    run = functools.partial(body, mesh.shape["section"], mesh.shape["dp"])
    return jax.shard_map(run, mesh=mesh, in_specs=in_specs, out_specs=out_specs, check_vma=False)
```

time: 107 us -> 47.2 us (0.44)
  the two profiles are of different devices: /device:TPU:0 before, /device:TPU:17 now
where the time goes in v1:
time: 47.2 us; the launch traced here: 47 us
  Pallas kernels  40.5 us (86%)
  local copies, waits for them, and re-layouts  5.8 us (12%)
  between operations  0.65 us (1%)
    pallas_call x1, Pallas kernels, body(): pl.pallas_call(functools.partial(kernel, S, N), out_shape=[jax.ShapeDtype...  40.5 us
    unnamed x6, local copies, waits for them, and re-layouts  5.8 us

profile of v1, /device:TPU:17, one launch (start us, length us, event | category | flops | bytes accessed | tf_op | source)
XLA Modules:
  0.0 47.0 jit_solution(3233076381446496371)
XLA Ops:
  0.6 40.5 %shard_map.93 = (f32[2,16,1536]{2,1,0:T(8,128)}, f32[2,16,1536]{2,1,0:T(8,128)}, f32[2,16,1536]{2,1,0:T(8,128)}, bf16[2,2,16,6144]{3,2,1,0:T(8,128)(2,1)}) custom-call(bf16[2,64,6144]{2,1,0:T(8,128)(2,1)} %bitcast.10, bf16[2,64,6144]{2,1,0:T(8,128)(2,1)} %bitcast.11, bf16[2,2,16,6144]{3,2,1,0:T(8,128)(2,1)} %bitcast.13, f32[2,16,1536]{2,1,0:T(8,128)} %bitcast.14, ...), custom_call_target="tpu_custom_call" | custom-call | tf_op jit(solution)/shard_map/pallas_call | solution.py:368
  41.2 0.0 copy-start
  41.2 1.7 %copy.14 = f32[1,2,16,1536]{3,2,1,0:T(8,128)} copy(f32[1,2,16,1536]{3,2,1,0:T(8,128)} %bitcast.19) | data formatting | bytes 393216
  42.9 1.6 %copy.15 = f32[1,2,16,1536]{3,2,1,0:T(8,128)} copy(f32[1,2,16,1536]{3,2,1,0:T(8,128)} %bitcast.18) | data formatting | bytes 393216
  44.5 1.6 %copy.16 = f32[1,2,16,1536]{3,2,1,0:T(8,128)} copy(f32[1,2,16,1536]{3,2,1,0:T(8,128)} %bitcast.17) | data formatting | bytes 393216
  46.1 0.0 copy-done
  46.1 0.9 %copy.17 = bf16[1,2,2,16,6144]{4,3,2,1,0:T(8,128)(2,1)} copy(bf16[1,2,2,16,6144]{4,3,2,1,0:T(8,128)(2,1)S(1)} %bitcast.12) | data formatting | bytes 1572864
Async XLA Ops:
  41.2 4.9 %copy-start = (bf16[2,2,16,6144]{3,2,1,0:T(8,128)(2,1)S(1)}, bf16[2,2,16,6144]{3,2,1,0:T(8,128)(2,1)}, u32[]{:S(2)}) copy-start(bf16[2,2,16,6144]{3,2,1,0:T(8,128)(2,1)} %get-tuple-element.11) | copy-start | bytes 2359300
